TPU v7x, 32 devices: a whole 2x2x4 slice. The times are simulated.
32 devices in a mesh: rep: 16 (over z, x, core), shard: 2 (over y).
Axes of the slice: x: 2, y: 2, z: 4, core: 2. Of those that a mesh axis runs over, the one named last changes fastest.
Arguments:
- tokens: bfloat16 [32, 197, 512], P(('rep', 'shard')), may hold values from -6 to 6
- norm_one: bfloat16 [512], P('shard'), may hold values from 0.099609375 to 1.8984375
- w_qkv: bfloat16 [512, 1536], P('shard'), may hold values from -0.25 to 0.25
- w_attn: bfloat16 [512, 512], P('shard'), may hold values from -1 to 1
- norm_two: bfloat16 [512], P('shard'), may hold values from 0.099609375 to 1.8984375
- w_gate: bfloat16 [512, 4], P('shard'), may hold values from -0.1875 to 0.1875
- w_expin: bfloat16 [4, 512, 2048], P(None, 'shard'), may hold values from -0.25 to 0.25
- w_expout: bfloat16 [4, 2048, 512], P(None, 'shard'), may hold values from -0.125 to 0.125
- routes: int32 [32, 197, 2], P(('rep', 'shard')), may hold values from 0 to 3, all different within a row
- cotangent: bfloat16 [32, 197, 512], P(('rep', 'shard')), may hold values from -6 to 6
Outputs:
- output: bfloat16 [32, 197, 512], P(('rep', 'shard'))
- grad_tokens: bfloat16 [32, 197, 512], P(('rep', 'shard'))
- grad_norm_one: float32 [512], P('shard')
- grad_qkv: float32 [512, 1536], P('shard')
- grad_attn: float32 [512, 512], P('shard')
- grad_norm_two: float32 [512], P('shard')
- grad_gate: float32 [512, 4], P('shard')
- grad_expin: float32 [4, 512, 2048], P(None, 'shard')
- grad_expout: float32 [4, 2048, 512], P(None, 'shard')
Inputs may be any that keep to these rules, and one draw needn't show every extreme that they name: `routes`: each token names two different experts; every expert is named by some token.
All inputs are finite; a program needn't handle non-finite values.
Results may differ from a plain program's by a relative error of at most 0.024.
Values may be sent and summed in bfloat16 or wider, within the bound.
A program may use at most 192 MiB of HBM per device.

v0:
```python
from functools import partial
import jax
import jax.numpy as jnp
from jax import lax
from jax.sharding import PartitionSpec as P

HEADS = 8
HEAD_DIM = 64
norm_eps = 1e-06
highest = lax.Precision.HIGHEST
fdt = jnp.float32
bdt = jnp.bfloat16


def layer_norm(inputs, gain_vec):
    centre = inputs - jnp.mean(inputs, axis=-1, keepdims=True)
    variance = jnp.mean(centre * centre, axis=-1, keepdims=True)
    inv_root = lax.rsqrt(variance + norm_eps)
    normed = centre * inv_root
    return (normed * gain_vec, normed, inv_root)


def norm_back(grad_out, normed, inv_root, gain_vec):
    scaled = grad_out * gain_vec
    back = inv_root * (
        scaled
        - jnp.mean(scaled, axis=-1, keepdims=True)
        - normed * jnp.mean(scaled * normed, axis=-1, keepdims=True)
    )
    return (back, jnp.sum(grad_out * normed, axis=0))


def forward(weights, tokens, routes, kept_total):
    norm_one, w_qkv, w_attn, norm_two, w_gate, w_expin, w_expout = weights
    images, seq_len, model_width = tokens.shape
    tok_rows = images * seq_len
    resid = tokens.reshape(tok_rows, model_width).astype(fdt)
    hidden_one, normed_one, root_one = layer_norm(resid, norm_one.astype(fdt))
    hidden_one_low = hidden_one.astype(bdt)
    proj = jnp.dot(hidden_one_low, w_qkv, preferred_element_type=fdt).astype(bdt)
    proj = proj.reshape(images, seq_len, 3, HEADS, HEAD_DIM)
    queries = proj[:, :, 0]
    key_rows = proj[:, :, 1]
    val_rows = proj[:, :, 2]
    score_scale = HEAD_DIM ** (-0.5)
    scores = (
        jnp.einsum("ishd,ithd->ihst", queries, key_rows, preferred_element_type=fdt) * score_scale
    )
    if kept_total is None:
        log_total = jax.nn.logsumexp(scores, axis=-1, keepdims=True)
    else:
        log_total = kept_total
    soft_probs = jnp.exp(scores - log_total)
    probs_low = soft_probs.astype(bdt)
    attn_rows = jnp.einsum("ihst,ithd->ishd", probs_low, val_rows, preferred_element_type=fdt)
    attn_rows = attn_rows.reshape(tok_rows, model_width).astype(bdt)
    mixed = resid + jnp.dot(attn_rows, w_attn, preferred_element_type=fdt)
    gate_gain = norm_two.astype(fdt)
    hidden_two, normed_two, root_two = layer_norm(mixed, gate_gain)
    router = w_gate.astype(fdt)
    logits = jnp.dot(hidden_two, router, precision=highest)
    expert_count = router.shape[1]
    choose = (
        routes.reshape(tok_rows, 2)[:, :, None] == jnp.arange(expert_count)[None, None, :]
    ).astype(fdt)
    picked = jnp.sum(choose * logits[:, None, :], axis=-1)
    gates = jax.nn.softmax(picked, axis=-1)
    weight_map = jnp.sum(gates[:, :, None] * choose, axis=1)
    hidden_two_low = hidden_two.astype(bdt)
    expert_inner = jnp.einsum("td,edf->etf", hidden_two_low, w_expin, preferred_element_type=fdt)
    hidden_act = jax.nn.gelu(expert_inner, approximate=False).astype(bdt)
    outer = jnp.einsum("etf,efd->etd", hidden_act, w_expout, preferred_element_type=fdt)
    combined = mixed + jnp.sum(weight_map.T[:, :, None] * outer, axis=0)
    return {
        "combined": combined,
        "log_total": log_total,
        "resid": resid,
        "normed_one": normed_one,
        "root_one": root_one,
        "hidden_one_low": hidden_one_low,
        "queries": queries,
        "key_rows": key_rows,
        "val_rows": val_rows,
        "soft_probs": soft_probs,
        "probs_low": probs_low,
        "attn_rows": attn_rows,
        "normed_two": normed_two,
        "root_two": root_two,
        "hidden_two": hidden_two,
        "hidden_two_low": hidden_two_low,
        "choose": choose,
        "gates": gates,
        "weight_map": weight_map,
        "expert_inner": expert_inner,
        "hidden_act": hidden_act,
        "outer": outer,
    }


def on_device(
    tokens, norm_one, w_qkv, w_attn, norm_two, w_gate, w_expin, w_expout, routes, cotangent
):
    images, seq_len, model_width = tokens.shape
    tok_rows = images * seq_len
    whole = (
        lax.all_gather(norm_one, "shard", axis=0, tiled=True),
        lax.all_gather(w_qkv, "shard", axis=0, tiled=True),
        lax.all_gather(w_attn, "shard", axis=0, tiled=True),
        lax.all_gather(norm_two, "shard", axis=0, tiled=True),
        lax.all_gather(w_gate, "shard", axis=0, tiled=True),
        lax.all_gather(w_expin, "shard", axis=1, tiled=True),
        lax.all_gather(w_expout, "shard", axis=1, tiled=True),
    )
    first = forward(whole, tokens, routes, None)
    output = first["combined"].reshape(images, seq_len, model_width).astype(bdt)
    again = (
        lax.all_gather(norm_one, "shard", axis=0, tiled=True),
        lax.all_gather(w_qkv, "shard", axis=0, tiled=True),
        lax.all_gather(w_attn, "shard", axis=0, tiled=True),
        lax.all_gather(norm_two, "shard", axis=0, tiled=True),
        lax.all_gather(w_gate, "shard", axis=0, tiled=True),
        lax.all_gather(w_expin, "shard", axis=1, tiled=True),
        lax.all_gather(w_expout, "shard", axis=1, tiled=True),
    )
    parts = forward(again, tokens, routes, first["log_total"])
    g_one, m_qkv, m_attn, g_two, m_gate, m_expin, m_expout = again
    gain_one = g_one.astype(fdt)
    gain_two = g_two.astype(fdt)
    router = m_gate.astype(fdt)
    dout = cotangent.reshape(tok_rows, model_width).astype(fdt)
    dweight = jnp.sum(dout[None, :, :] * parts["outer"], axis=-1).T
    dout_exp = (parts["weight_map"].T[:, :, None] * dout[None, :, :]).astype(bdt)
    grad_expout = jnp.einsum(
        "etf,etd->efd", parts["hidden_act"], dout_exp, preferred_element_type=fdt
    )
    dhidden = jnp.einsum("etd,efd->etf", dout_exp, m_expout, preferred_element_type=fdt)
    gelu_exact = partial(jax.nn.gelu, approximate=False)
    _, gelu_pull = jax.vjp(gelu_exact, parts["expert_inner"])
    dinner = gelu_pull(dhidden)[0].astype(bdt)
    grad_expin = jnp.einsum(
        "td,etf->edf", parts["hidden_two_low"], dinner, preferred_element_type=fdt
    )
    dhidden_two = jnp.einsum("etf,edf->td", dinner, m_expin, preferred_element_type=fdt)
    choose = parts["choose"]
    gates = parts["gates"]
    dpicked = jnp.sum(choose * dweight[:, None, :], axis=-1)
    gate_dot = jnp.sum(gates * dpicked, axis=-1, keepdims=True)
    dpair = gates * (dpicked - gate_dot)
    dlogits = jnp.sum(dpair[:, :, None] * choose, axis=1)
    grad_gate = jnp.dot(parts["hidden_two"].T, dlogits, precision=highest)
    dhidden_two = dhidden_two + jnp.dot(dlogits, router.T, precision=highest)
    dmixed_norm, grad_norm_two = norm_back(
        dhidden_two, parts["normed_two"], parts["root_two"], gain_two
    )
    dmixed = dout + dmixed_norm
    dmixed_low = dmixed.astype(bdt)
    grad_attn = jnp.dot(parts["attn_rows"].T, dmixed_low, preferred_element_type=fdt)
    dattn = jnp.dot(dmixed_low, m_attn.T, preferred_element_type=fdt).astype(bdt)
    dattn = dattn.reshape(images, seq_len, HEADS, HEAD_DIM)
    dprobs = jnp.einsum("ishd,ithd->ihst", dattn, parts["val_rows"], preferred_element_type=fdt)
    dvalues = jnp.einsum("ihst,ishd->ithd", parts["probs_low"], dattn, preferred_element_type=fdt)
    soft_probs = parts["soft_probs"]
    row_delta = jnp.sum(dprobs * soft_probs, axis=-1, keepdims=True)
    dscores = (soft_probs * (dprobs - row_delta)).astype(bdt)
    score_scale = HEAD_DIM ** (-0.5)
    dqueries = (
        jnp.einsum("ihst,ithd->ishd", dscores, parts["key_rows"], preferred_element_type=fdt)
        * score_scale
    )
    dkeys = (
        jnp.einsum("ihst,ishd->ithd", dscores, parts["queries"], preferred_element_type=fdt)
        * score_scale
    )
    dproj = (
        jnp.stack([dqueries, dkeys, dvalues], axis=2).reshape(tok_rows, 3 * model_width).astype(bdt)
    )
    grad_qkv = jnp.dot(parts["hidden_one_low"].T, dproj, preferred_element_type=fdt)
    dhidden_one = jnp.dot(dproj, m_qkv.T, preferred_element_type=fdt)
    dresid_norm, grad_norm_one = norm_back(
        dhidden_one, parts["normed_one"], parts["root_one"], gain_one
    )
    grad_tokens = (dmixed + dresid_norm).reshape(images, seq_len, model_width).astype(bdt)
    owned = (
        lax.psum_scatter(
            grad_norm_one.astype(jnp.bfloat16), "shard", scatter_dimension=0, tiled=True
        ).astype(jnp.float32),
        lax.psum_scatter(
            grad_qkv.astype(jnp.bfloat16), "shard", scatter_dimension=0, tiled=True
        ).astype(jnp.float32),
        lax.psum_scatter(
            grad_attn.astype(jnp.bfloat16), "shard", scatter_dimension=0, tiled=True
        ).astype(jnp.float32),
        lax.psum_scatter(
            grad_norm_two.astype(jnp.bfloat16), "shard", scatter_dimension=0, tiled=True
        ).astype(jnp.float32),
        lax.psum_scatter(
            grad_gate.astype(jnp.bfloat16), "shard", scatter_dimension=0, tiled=True
        ).astype(jnp.float32),
        lax.psum_scatter(
            grad_expin.astype(jnp.bfloat16), "shard", scatter_dimension=1, tiled=True
        ).astype(jnp.float32),
        lax.psum_scatter(
            grad_expout.astype(jnp.bfloat16), "shard", scatter_dimension=1, tiled=True
        ).astype(jnp.float32),
    )
    summed = (
        lax.psum(owned[0].astype(jnp.bfloat16), "rep").astype(jnp.float32),
        lax.psum(owned[1].astype(jnp.bfloat16), "rep").astype(jnp.float32),
        lax.psum(owned[2].astype(jnp.bfloat16), "rep").astype(jnp.float32),
        lax.psum(owned[3].astype(jnp.bfloat16), "rep").astype(jnp.float32),
        lax.psum(owned[4].astype(jnp.bfloat16), "rep").astype(jnp.float32),
        lax.psum(owned[5].astype(jnp.bfloat16), "rep").astype(jnp.float32),
        lax.psum(owned[6].astype(jnp.bfloat16), "rep").astype(jnp.float32),
    )
    return (
        output,
        grad_tokens,
        summed[0],
        summed[1],
        summed[2],
        summed[3],
        summed[4],
        summed[5],
        summed[6],
    )


def solution(mesh):
    placed = (
        P(("rep", "shard"), None, None),
        P("shard"),
        P("shard", None),
        P("shard", None),
        P("shard"),
        P("shard", None),
        P(None, "shard", None),
        P(None, "shard", None),
        P(("rep", "shard"), None, None),
        P(("rep", "shard"), None, None),
    )
    return jax.shard_map(
        on_device,
        mesh=mesh,
        in_specs=placed,
        out_specs=(
            P(("rep", "shard"), None, None),
            P(("rep", "shard"), None, None),
            P("shard"),
            P("shard", None),
            P("shard", None),
            P("shard"),
            P("shard", None),
            P(None, "shard", None),
            P(None, "shard", None),
        ),
        check_vma=False,
    )
```

profile of v0, /device:TPU:0, one launch (start us, length us, event | category | flops | bytes accessed | tf_op | source)
XLA Modules:
  0.0 764.5 jit_solution(5038029769242780368)
XLA Ops:
  9.7 5.2 all-gather
  14.8 4.2 all-gather.1
  19.1 4.3 all_gather.32
  23.7 14.0 %all_gather.30 = bf16[512,512]{1,0:T(8,128)(2,1)} all-gather(bf16[256,512]{1,0:T(8,128)(2,1)S(1)} %copy-done.11), channel_id=1, replica_groups=mesh['rep'=16,'shard'=2] {'shard'}, dimensions={0}, use_global_device_ids=true | all-gather | bytes 786432 | tf_op jit(solution)/shard_map/all_gather | solution.py:108
  38.5 6.7 all-gather.6.cloned.1.call-done
  45.2 1.9 convolution_convert_fusion.2
  49.3 1.4 fusion.76
  51.5 99.3 %all-gather.8.cloned.1.call-done = bf16[4,512,2048]{2,1,0:T(8,128)(2,1)} async-done(((bf16[4,256,2048]{2,1,0:T(8,128)(2,1)}), bf16[4,512,2048]{2,1,0:T(8,128)(2,1)}) %all-gather.8.cloned.1.call-update) | async-done | bytes 8388624 | tf_op jit(solution)/shard_map/all_gather | solution.py:111
  150.8 18.8 %fusion.2 = (bf16[4,197,2048]{2,1,0:T(8,128)(2,1)}, f32[4,197,2048]{2,1,0:T(8,128)}, f32[197,4,2048]{2,0,1:T(8,128)}) fusion(bf16[4,512,2048]{2,1,0:T(8,128)(2,1)} %all-gather.8.cloned.1.call-done, f32[512]{0:T(512)S(1)} %bitcast.219, f32[197]{0:T(256)S(1)} %add_rsqrt_fusion, f32[197,512]{1,0:T(8,128)S(1)} %get-tuple-element.69, ...), kind=kOutput, calls=%fused_computation.10 | convolution fusion | flops 1757857792 | bytes 24933928 | tf_op jit(solution)/shard_map/td,edf->etf/dot_general | solution.py:70
  169.6 86.8 %all-gather.10.cloned.1.call-done = bf16[4,2048,512]{2,1,0:T(8,128)(2,1)} async-done(((bf16[4,1024,512]{2,1,0:T(8,128)(2,1)}), bf16[4,2048,512]{2,1,0:T(8,128)(2,1)}) %all-gather.10.cloned.1.call-update) | async-done | bytes 8388624 | tf_op jit(solution)/shard_map/all_gather | solution.py:112
  256.4 6.5 multiply_reduce_fusion.1
  263.0 11.2 %fusion.8 = bf16[4,197,2048]{2,1,0:T(8,128)(2,1)S(1)} fusion(f32[4,197,2048]{2,1,0:T(8,128)} %get-tuple-element.63, f32[197,4,2048]{2,0,1:T(8,128)} %get-tuple-element.70, bf16[4,2048,512]{2,1,0:T(8,128)(2,1)} %all-gather.10.cloned.1.call-done, f32[197,512]{1,0:T(8,128)S(1)} %copy-done.6, f32[4,197]{1,0:T(4,128)S(1)} %bitcast.233), kind=kOutput, calls=%fused_computation.16 | convolution fusion | flops 1675956224 | bytes 24933456 | tf_op jit(solution)/shard_map/etd,efd->etf/dot_general | solution.py:136
  274.3 7.4 convolution_bitcast_fusion.1
  283.1 1.0 convolution_convert_fusion.5
  284.1 1.1 convolution_convert_fusion.3
  285.2 1.8 copy.52
  287.0 2.6 multiply_reduce_fusion
  289.9 1.9 multiply_convert_fusion
  293.0 1.9 convolution_convert_fusion.1
  295.0 8.1 %convert_bitcast_fusion = bf16[4,512,2048]{1,2,0:T(8,128)(2,1)} fusion(bf16[4,197,2048]{2,1,0:T(8,128)(2,1)} %copy-done.1, f32[512]{0:T(512)S(1)} %bitcast.222, f32[197,512]{1,0:T(8,128)S(1)} %get-tuple-element.69, f32[197]{0:T(256)S(1)} %add_rsqrt_fusion, f32[197]{0:T(256)S(1)} %broadcast_multiply_fusion.4), kind=kOutput, calls=%fused_computation.1 | convolution fusion | flops 1657153536 | bytes 12023336 | tf_op jit(solution)/shard_map/td,etf->edf/dot_general | solution.py:140
  304.1 7.9 %convolution_convert_fusion = bf16[4,2048,512]{2,1,0:T(8,128)(2,1)} fusion(bf16[4,197,2048]{2,1,0:T(8,128)(2,1)} %get-tuple-element.62, f32[197,512]{1,0:T(8,128)S(1)} %copy-done.7, f32[4,197]{1,0:T(4,128)S(1)} %bitcast.234), kind=kOutput, calls=%fused_computation.30 | convolution fusion | flops 1657556992 | bytes 12022864 | tf_op jit(solution)/shard_map/etf,etd->efd/dot_general | solution.py:133
  313.4 19.7 %reduce-scatter.8.cloned.1.call-done = bf16[256,1536]{1,0:T(8,128)(2,1)} async-done(((bf16[512,1536]{1,0:T(8,128)(2,1)}), bf16[256,1536]{1,0:T(8,128)(2,1)}) %reduce-scatter.8.cloned.1.call-update) | async-done | bytes 786448 | tf_op jit(solution)/shard_map/reduce_scatter | solution.py:187
  333.2 102.0 %reduce-scatter.12.cloned.1.call-done = bf16[4,256,2048]{1,2,0:T(8,128)(2,1)} async-done(((bf16[4,512,2048]{1,2,0:T(8,128)(2,1)}), bf16[4,256,2048]{1,2,0:T(8,128)(2,1)}) %reduce-scatter.12.cloned.1.call-update) | async-done | bytes 4194320 | tf_op jit(solution)/shard_map/reduce_scatter | solution.py:199
  435.2 102.2 %reduce-scatter.14.cloned.1.call-done = bf16[4,1024,512]{2,1,0:T(8,128)(2,1)} async-done(((bf16[4,2048,512]{2,1,0:T(8,128)(2,1)}), bf16[4,1024,512]{2,1,0:T(8,128)(2,1)}) %reduce-scatter.14.cloned.1.call-update) | async-done | bytes 4194320 | tf_op jit(solution)/shard_map/reduce_scatter | solution.py:202
  539.5 4.9 all-reduce.4
  545.5 4.4 reduce-scatter.16.cloned.1.call-done
  550.9 34.5 %all-reduce.2 = (bf16[256]{0:T(256)(128)(2,1)S(1)}, bf16[256]{0:T(256)(128)(2,1)S(1)}, bf16[256,4]{0,1:T(4,128)(2,1)S(1)}) all-reduce(bf16[256]{0:T(256)(128)(2,1)S(1)} %dynamic-slice.1, bf16[256]{0:T(256)(128)(2,1)S(1)} %dynamic-slice.3, bf16[256,4]{0,1:T(4,128)(2,1)S(1)} %copy.62), channel_id=1, replica_groups=mesh['rep'=16,'shard'=2] {'rep'}, use_global_device_ids=true, to_apply=%region_22.0 | all-reduce | flops 1536 | bytes 6144 | tf_op jit(solution)/shard_map/psum | solution.py:207
  587.1 153.0 %all-reduce.7.cloned.1.call-done = (bf16[4,256,2048]{1,2,0:T(8,128)(2,1)}, bf16[256,1536]{1,0:T(8,128)(2,1)}, bf16[256,512]{1,0:T(8,128)(2,1)}, bf16[4,1024,512]{2,1,0:T(8,128)(2,1)}) async-done(((bf16[4,256,2048]{1,2,0:T(8,128)(2,1)}, bf16[256,1536]{1,0:T(8,128)(2,1)}, bf16[256,512]{1,0:T(8,128)(2,1)}, bf16[4,1024,512]{2,1,0:T(8,128)(2,1)}), (bf16[4,256,2048]{1,2,0:T(8,128)(2,1)}, ...) | async-done | bytes 9437200 | tf_op jit(solution)/shard_map/psum | solution.py:212
  740.0 2.5 convert_element_type.206
  742.5 1.8 convert_element_type.208
  744.3 6.9 copy.56
  751.2 6.8 convert_element_type.217
  (101 shorter events, 16.9 us)
Async XLA Ops:
  7.2 2.3 copy-start
  7.2 2.4 copy-start.14
  7.2 7.6 copy-start.15
  7.2 11.9 %copy-start.13 = (bf16[256,4]{0,1:T(4,128)(2,1)S(1)}, bf16[256,4]{0,1:T(4,128)(2,1)}, u32[]{:S(2)}) copy-start(bf16[256,4]{0,1:T(4,128)(2,1)} %param.15) | copy-start | bytes 6148
  7.2 16.4 %copy-start.11 = (bf16[256,512]{1,0:T(8,128)(2,1)S(1)}, bf16[256,512]{1,0:T(8,128)(2,1)}, u32[]{:S(2)}) copy-start(bf16[256,512]{1,0:T(8,128)(2,1)} %param.13) | copy-start | bytes 786436
  7.2 30.5 %copy-start.9 = (bf16[1,197,512]{2,1,0:T(8,128)(2,1)S(1)}, bf16[1,197,512]{2,1,0:T(8,128)(2,1)}, u32[]{:S(2)}) copy-start(bf16[1,197,512]{2,1,0:T(8,128)(2,1)} %param.19) | copy-start | bytes 605188
  7.2 38.0 %all-gather.6.cloned.1.call-start = ((), (), s32[]{:S(2)}) async-start(), calls=%async_computation.5 | async-start | bytes 2359296 | tf_op jit(solution)/shard_map/all_gather | solution.py:107
  8.0 142.8 %all-gather.8.cloned.1.call-start = ((), (), s32[]{:S(2)}) async-start(), calls=%async_computation.6 | async-start | bytes 12582912 | tf_op jit(solution)/shard_map/all_gather | solution.py:111
  8.7 247.7 %all-gather.10.cloned.1.call-start = ((), (), s32[]{:S(2)}) async-start(), calls=%async_computation.7 | async-start | bytes 12582912 | tf_op jit(solution)/shard_map/all_gather | solution.py:112
  9.5 304.0 %reduce-scatter.10.cloned.1.call-start = ((), (), s32[]{:S(2)}) async-start(), calls=%async_computation.9 | async-start | bytes 786432 | tf_op jit(solution)/shard_map/reduce_scatter | solution.py:190
  23.7 27.7 %copy-start.12 = (s32[1,197,2]{1,2,0:T(2,128)S(1)}, s32[1,197,2]{1,2,0:T(2,128)}, u32[]{:S(2)}) copy-start(s32[1,197,2]{1,2,0:T(2,128)} %param.18) | copy-start | bytes 4732
  48.6 0.7 copy-start.3
  51.5 204.9 %copy-start.6 = (f32[197,512]{1,0:T(8,128)S(1)}, f32[197,512]{1,0:T(8,128)}, u32[]{:S(2)}) copy-start(f32[197,512]{1,0:T(8,128)} %bitcast_convert_fusion) | copy-start | bytes 1210372
  274.2 7.5 copy-start.1
  274.2 8.1 %copy-start.10 = (bf16[1,197,512]{2,1,0:T(8,128)(2,1)S(1)}, bf16[1,197,512]{2,1,0:T(8,128)(2,1)}, u32[]{:S(2)}) copy-start(bf16[1,197,512]{2,1,0:T(8,128)(2,1)} %param.19) | copy-start | bytes 605188
  274.2 8.9 %copy-start.2 = (bf16[512,512]{1,0:T(8,128)(2,1)S(1)}, bf16[512,512]{1,0:T(8,128)(2,1)}, u32[]{:S(2)}) copy-start(bf16[512,512]{1,0:T(8,128)(2,1)} %all_gather.30) | copy-start | bytes 1572868
  274.2 9.9 %copy-start.4 = (bf16[8,64,197]{2,1,0:T(8,128)(2,1)S(1)}, bf16[8,64,197]{2,1,0:T(8,128)(2,1)}, u32[]{:S(2)}) copy-start(bf16[8,64,197]{2,1,0:T(8,128)(2,1)} %copy-done.3) | copy-start | bytes 605188
  289.6 43.6 %reduce-scatter.8.cloned.1.call-start = ((), (), s32[]{:S(2)}) async-start(), calls=%async_computation.8 | async-start | bytes 2359296 | tf_op jit(solution)/shard_map/reduce_scatter | solution.py:187
  289.8 2.6 copy-start.5
  294.9 140.2 %reduce-scatter.12.cloned.1.call-start = ((), (), s32[]{:S(2)}) async-start(), calls=%async_computation.10 | async-start | bytes 12582912 | tf_op jit(solution)/shard_map/reduce_scatter | solution.py:199
  303.1 1.0 copy-start.7
  303.1 234.3 %reduce-scatter.14.cloned.1.call-start = ((), (), s32[]{:S(2)}) async-start(), calls=%async_computation.11 | async-start | bytes 12582912 | tf_op jit(solution)/shard_map/reduce_scatter | solution.py:202
  312.0 225.4 %copy-start.16 = (u32[32]{0:T(128)S(1)}, u32[32]{0:T(128)}, u32[]{:S(2)}) copy-start(u32[32]{0:T(128)} %constant.92) | copy-start | bytes 388
  312.0 226.7 %copy-start.8 = (bf16[512,1536]{1,0:T(8,128)(2,1)S(1)}, bf16[512,1536]{1,0:T(8,128)(2,1)}, u32[]{:S(2)}) copy-start(bf16[512,1536]{1,0:T(8,128)(2,1)} %all-gather.6.cloned.1.call-done) | copy-start | bytes 4718596
  312.0 237.9 %reduce-scatter.16.cloned.1.call-start = ((), (), s32[]{:S(2)}) async-start(), calls=%async_computation.12 | async-start | bytes 196608
  313.3 426.7 %all-reduce.7.cloned.1.call-start = ((), (), s32[]{:S(2)}) async-start(), calls=%async_computation.13 | async-start | bytes 18874368 | tf_op jit(solution)/shard_map/psum | solution.py:212
Sparse Core Ops, SparseCore 0:
  9.6 35.5 all-gather.5
  46.7 103.9 all-gather.7
  152.3 103.9 all-gather.9
  289.7 14.5 reduce-scatter.9
  307.0 26.0 reduce-scatter.7
  335.9 99.2 reduce-scatter.11
  438.1 99.2 reduce-scatter.13
  539.6 10.2 reduce-scatter.15
  553.9 186.0 all-reduce.6
where the time goes:
time: 765 us; the launch traced here: 764 us
  waiting for transfers between devices  576 us (75%)
  matrix products  74.1 us (10%)
  blocking collectives  67.2 us (9%)
  other arithmetic  18.4 us (2%)
  between operations  14.8 us (2%)
  local copies, waits for them, and re-layouts  13.1 us (2%)
    psum x1, waiting for transfers between devices, on_device(): lax.psum(owned[5].astype(jnp.bfloat16), 'rep').astype(jnp.float32)  153 us
    reduce_scatter x1, waiting for transfers between devices, on_device(): lax.psum_scatter(grad_expout.astype(jnp.bfloat16), 'shard', scatter_dimen...  102 us
    reduce_scatter x1, waiting for transfers between devices, on_device(): lax.psum_scatter(grad_expin.astype(jnp.bfloat16), 'shard', scatter_dimens...  102 us
    all_gather x1, waiting for transfers between devices, on_device(): lax.all_gather(w_expin, 'shard', axis=1, tiled=True)  99.3 us
    all_gather x1, waiting for transfers between devices, on_device(): lax.all_gather(w_expout, 'shard', axis=1, tiled=True)  86.8 us
    psum x1, blocking collectives, on_device(): lax.psum(owned[0].astype(jnp.bfloat16), 'rep').astype(jnp.float32)  34.5 us
    reduce_scatter x1, waiting for transfers between devices, on_device(): lax.psum_scatter(grad_qkv.astype(jnp.bfloat16), 'shard', scatter_dimensio...  19.7 us
    dot_general x1, matrix products, forward(): jnp.einsum('td,edf->etf', hidden_two_low, w_expin, preferred_element_type...  18.8 us
  transfers between devices with their start and end apart: 9, of which 8 were waited for; matrix products, arithmetic and copies ran while one was open for 7% of the time, Pallas kernels for 0%

commit v1 on v0

--- a/solution.py
+++ b/solution.py
@@ -102,6 +102,20 @@
 ):
     images, seq_len, model_width = tokens.shape
     tok_rows = images * seq_len
+
+    def wrap_body(chunk, dev_axis, along_dim):
+        out_arr = lax.axis_index(dev_axis)
+        finding = lax.axis_size(dev_axis)
+        x_new, w2, current_arr = (finding, out_arr, chunk.shape[along_dim])
+        known, low = (chunk, 1)
+        while low < x_new:
+            block_out = lax.ppermute(
+                known, dev_axis, [(idx, (idx - low) % x_new) for idx in range(x_new)]
+            )
+            known = jnp.concatenate([known, block_out], axis=along_dim)
+            low = 2 * low
+        return jnp.roll(known, w2 * current_arr, axis=along_dim)
+
     whole = (
         lax.all_gather(norm_one, "shard", axis=0, tiled=True),
         lax.all_gather(w_qkv, "shard", axis=0, tiled=True),
@@ -109,7 +123,7 @@
         lax.all_gather(norm_two, "shard", axis=0, tiled=True),
         lax.all_gather(w_gate, "shard", axis=0, tiled=True),
         lax.all_gather(w_expin, "shard", axis=1, tiled=True),
-        lax.all_gather(w_expout, "shard", axis=1, tiled=True),
+        wrap_body(w_expout, "shard", 1),
     )
     first = forward(whole, tokens, routes, None)
     output = first["combined"].reshape(images, seq_len, model_width).astype(bdt)

time: 765 us -> 842 us (1.10)
  blocking collectives: 67.2 us -> 220 us
  waiting for transfers between devices: 576 us -> 487 us
  matrix products: 74.1 us -> 83.7 us
    all_gather x1, blocking collectives: 5.16 us -> 158 us  [on_device(): lax.all_gather(norm_one, 'shard', axis=0, tiled=True)]
    all_gather x1, waiting for transfers between devices: 99.3 us -> 15.8 us  [on_device(): lax.all_gather(w_expin, 'shard', axis=1, tiled=True)]
    dot_general x1 -> x2, matrix products: 6.5 us -> 16 us  [forward(): jnp.einsum('etf,efd->etd', hidden_act, w_expout, preferred_element_type=fdt)]
  transfers between devices with their start and end apart: 9 -> 10, of which waited for: 8 -> 7; matrix products, arithmetic and copies ran while one was open for 7% -> 9% of each run, Pallas kernels for 0% -> 0%
where the time goes in v1:
time: 842 us; the launch traced here: 841 us
  waiting for transfers between devices  487 us (58%)
  blocking collectives  220 us (26%)
  matrix products  83.7 us (10%)
  other arithmetic  18.3 us (2%)
  between operations  14.9 us (2%)
  local copies, waits for them, and re-layouts  13.1 us (2%)
    all_gather x1, blocking collectives, on_device(): lax.all_gather(norm_one, 'shard', axis=0, tiled=True)  158 us
    psum x1, waiting for transfers between devices, on_device(): lax.psum(owned[5].astype(jnp.bfloat16), 'rep').astype(jnp.float32)  153 us
    reduce_scatter x1, waiting for transfers between devices, on_device(): lax.psum_scatter(grad_expout.astype(jnp.bfloat16), 'shard', scatter_dimen...  102 us
    reduce_scatter x1, waiting for transfers between devices, on_device(): lax.psum_scatter(grad_expin.astype(jnp.bfloat16), 'shard', scatter_dimens...  102 us
    all_gather x1, waiting for transfers between devices, on_device(): lax.all_gather(w_expout, 'shard', axis=1, tiled=True)  88.2 us
    psum x1, blocking collectives, on_device(): lax.psum(owned[0].astype(jnp.bfloat16), 'rep').astype(jnp.float32)  34.5 us
    reduce_scatter x1, waiting for transfers between devices, on_device(): lax.psum_scatter(grad_qkv.astype(jnp.bfloat16), 'shard', scatter_dimensio...  19.7 us
    dot_general x1, matrix products, forward(): jnp.einsum('td,edf->etf', hidden_two_low, w_expin, preferred_element_type...  18.8 us
  transfers between devices with their start and end apart: 10, of which 7 were waited for; matrix products, arithmetic and copies ran while one was open for 9% of the time, Pallas kernels for 0%

profile of v1, /device:TPU:0, one launch (start us, length us, event | category | flops | bytes accessed | tf_op | source)
XLA Modules:
  0.0 840.8 jit_solution(4942526393530975611)
XLA Ops:
  9.5 3.0 collective-permute-start
  12.5 157.6 %all-gather = bf16[2,1,256]{2,1,0:T(2,128)(2,1)S(1)} all-gather(bf16[1,1,256]{2,1,0:T(2,128)(2,1)S(1)} %reshape.328), channel_id=1, replica_groups=mesh['rep'=16,'shard'=2] {'shard'}, dimensions={0}, use_global_device_ids=true | all-gather | bytes 1536 | tf_op jit(solution)/shard_map/all_gather | solution.py:120
  170.2 4.7 all-gather.1
  174.9 4.3 all_gather.31
  179.6 13.7 %all_gather.29 = bf16[512,512]{1,0:T(8,128)(2,1)} all-gather(bf16[256,512]{1,0:T(8,128)(2,1)S(1)} %copy-done.13), channel_id=1, replica_groups=mesh['rep'=16,'shard'=2] {'shard'}, dimensions={0}, use_global_device_ids=true | all-gather | bytes 786432 | tf_op jit(solution)/shard_map/all_gather | solution.py:122
  194.1 1.9 convolution_convert_fusion.2
  198.1 1.4 fusion.86
  200.2 15.8 %all-gather.8.cloned.1.call-done = bf16[4,512,2048]{2,1,0:T(8,128)(2,1)} async-done(((bf16[4,256,2048]{2,1,0:T(8,128)(2,1)}), bf16[4,512,2048]{2,1,0:T(8,128)(2,1)}) %all-gather.8.cloned.1.call-update) | async-done | bytes 8388624 | tf_op jit(solution)/shard_map/all_gather | solution.py:125
  216.0 18.8 %fusion.7 = (bf16[4,197,2048]{2,1,0:T(8,128)(2,1)}, f32[4,197,2048]{2,1,0:T(8,128)}, f32[197,4,2048]{2,0,1:T(8,128)}) fusion(bf16[4,512,2048]{2,1,0:T(8,128)(2,1)} %all-gather.8.cloned.1.call-done, f32[512]{0:T(512)S(1)} %bitcast.220, f32[197]{0:T(256)S(1)} %add_rsqrt_fusion, f32[197,512]{1,0:T(8,128)S(1)} %get-tuple-element.73, ...), kind=kOutput, calls=%fused_computation.18 | convolution fusion | flops 1757857792 | bytes 24933928 | tf_op jit(solution)/shard_map/td,edf->etf/dot_general | solution.py:70
  234.8 88.2 %all-gather.10.cloned.1.call-done = bf16[4,2048,512]{2,1,0:T(8,128)(2,1)} async-done(((bf16[4,1024,512]{2,1,0:T(8,128)(2,1)}), bf16[4,2048,512]{2,1,0:T(8,128)(2,1)}) %all-gather.10.cloned.1.call-update) | async-done | bytes 8388624 | tf_op jit(solution)/shard_map/all_gather | solution.py:137
  323.1 6.4 multiply_reduce_fusion.1
  329.6 11.2 %fusion.13 = bf16[4,197,2048]{2,1,0:T(8,128)(2,1)S(1)} fusion(f32[4,197,2048]{2,1,0:T(8,128)} %get-tuple-element.67, f32[197,4,2048]{2,0,1:T(8,128)} %get-tuple-element.74, bf16[4,2048,512]{2,1,0:T(8,128)(2,1)} %all-gather.10.cloned.1.call-done, f32[197,512]{1,0:T(8,128)S(1)} %copy-done.8, f32[4,197]{1,0:T(4,128)S(1)} %bitcast.229), kind=kOutput, calls=%fused_computation.24 | convolution fusion | flops 1675956224 | bytes 24933456 | tf_op jit(solution)/shard_map/etd,efd->etf/dot_general | solution.py:150
  340.9 7.4 convolution_bitcast_fusion.1
  348.9 9.7 %multiply_reduce_fusion.2 = f32[197,512]{1,0:T(8,128)S(1)} fusion(bf16[4,197,2048]{2,1,0:T(8,128)(2,1)S(1)} %copy-done.4, s32[]{:T(128)S(6)} %select_n.26, bf16[4,1024,512]{2,1,0:T(8,128)(2,1)S(1)} %copy-done.3, bf16[4,1024,512]{2,1,0:T(8,128)(2,1)} %collective-permute-done, f32[4,197]{1,0:T(4,128)S(1)} %bitcast.230), kind=kOutput, calls=%fused_computation.45 | convolution fusion | flops 1686816256 | bytes 12022868 | tf_op jit(solution)/shard_map/etf,efd->etd/dot_general | solution.py:72
  360.5 1.1 convolution_convert_fusion.3
  361.6 1.8 copy.52
  363.3 2.6 multiply_reduce_fusion
  366.0 1.9 multiply_convert_fusion
  369.1 1.9 convolution_convert_fusion.1
  371.1 8.2 convert_bitcast_fusion
  380.3 7.9 convolution_convert_fusion
  389.9 19.7 %reduce-scatter.8.cloned.1.call-done = bf16[256,1536]{1,0:T(8,128)(2,1)} async-done(((bf16[512,1536]{1,0:T(8,128)(2,1)}), bf16[256,1536]{1,0:T(8,128)(2,1)}) %reduce-scatter.8.cloned.1.call-update) | async-done | bytes 786448 | tf_op jit(solution)/shard_map/reduce_scatter | solution.py:201
  409.5 102.0 %reduce-scatter.12.cloned.1.call-done = bf16[4,256,2048]{1,2,0:T(8,128)(2,1)} async-done(((bf16[4,512,2048]{1,2,0:T(8,128)(2,1)}), bf16[4,256,2048]{1,2,0:T(8,128)(2,1)}) %reduce-scatter.12.cloned.1.call-update) | async-done | bytes 4194320 | tf_op jit(solution)/shard_map/reduce_scatter | solution.py:213
  511.5 102.2 %reduce-scatter.14.cloned.1.call-done = bf16[4,1024,512]{2,1,0:T(8,128)(2,1)} async-done(((bf16[4,2048,512]{2,1,0:T(8,128)(2,1)}), bf16[4,1024,512]{2,1,0:T(8,128)(2,1)}) %reduce-scatter.14.cloned.1.call-update) | async-done | bytes 4194320 | tf_op jit(solution)/shard_map/reduce_scatter | solution.py:216
  615.9 4.9 all-reduce.4
  621.9 4.4 reduce-scatter.16.cloned.1.call-done
  627.2 34.5 %all-reduce.2 = (bf16[256]{0:T(256)(128)(2,1)S(1)}, bf16[256]{0:T(256)(128)(2,1)S(1)}, bf16[256,4]{0,1:T(4,128)(2,1)S(1)}) all-reduce(bf16[256]{0:T(256)(128)(2,1)S(1)} %dynamic-slice.1, bf16[256]{0:T(256)(128)(2,1)S(1)} %dynamic-slice.3, bf16[256,4]{0,1:T(4,128)(2,1)S(1)} %copy.62), channel_id=1, replica_groups=mesh['rep'=16,'shard'=2] {'rep'}, use_global_device_ids=true, to_apply=%region_22.23 | all-reduce | flops 1536 | bytes 6144 | tf_op jit(solution)/shard_map/psum | solution.py:221
  663.5 152.9 %all-reduce.7.cloned.1.call-done = (bf16[4,256,2048]{1,2,0:T(8,128)(2,1)}, bf16[256,1536]{1,0:T(8,128)(2,1)}, bf16[256,512]{1,0:T(8,128)(2,1)}, bf16[4,1024,512]{2,1,0:T(8,128)(2,1)}) async-done(((bf16[4,256,2048]{1,2,0:T(8,128)(2,1)}, bf16[256,1536]{1,0:T(8,128)(2,1)}, bf16[256,512]{1,0:T(8,128)(2,1)}, bf16[4,1024,512]{2,1,0:T(8,128)(2,1)}), (bf16[4,256,2048]{1,2,0:T(8,128)(2,1)}, ...) | async-done | bytes 9437200 | tf_op jit(solution)/shard_map/psum | solution.py:226
  816.4 2.5 convert_element_type.206
  818.8 1.8 convert_element_type.208
  820.6 6.9 copy.56
  827.5 6.8 convert_element_type.217
  (105 shorter events, 17.8 us)
Async XLA Ops:
  7.2 5.4 copy-start.16
  7.2 163.0 %copy-start.17 = (bf16[256]{0:T(256)(128)(2,1)S(1)}, bf16[256]{0:T(256)(128)(2,1)}, u32[]{:S(2)}) copy-start(bf16[256]{0:T(256)(128)(2,1)} %param.14) | copy-start | bytes 1540
  7.2 167.7 %copy-start.15 = (bf16[256,4]{0,1:T(4,128)(2,1)S(1)}, bf16[256,4]{0,1:T(4,128)(2,1)}, u32[]{:S(2)}) copy-start(bf16[256,4]{0,1:T(4,128)(2,1)} %param.15) | copy-start | bytes 6148
  7.2 172.0 %copy-start = (bf16[1,197,512]{2,1,0:T(8,128)(2,1)S(1)}, bf16[1,197,512]{2,1,0:T(8,128)(2,1)}, u32[]{:S(2)}) copy-start(bf16[1,197,512]{2,1,0:T(8,128)(2,1)} %param.10) | copy-start | bytes 605188
  7.2 172.3 %copy-start.13 = (bf16[256,512]{1,0:T(8,128)(2,1)S(1)}, bf16[256,512]{1,0:T(8,128)(2,1)}, u32[]{:S(2)}) copy-start(bf16[256,512]{1,0:T(8,128)(2,1)} %param.13) | copy-start | bytes 786436
  7.2 186.0 %copy-start.11 = (bf16[1,197,512]{2,1,0:T(8,128)(2,1)S(1)}, bf16[1,197,512]{2,1,0:T(8,128)(2,1)}, u32[]{:S(2)}) copy-start(bf16[1,197,512]{2,1,0:T(8,128)(2,1)} %param.19) | copy-start | bytes 605188
  7.2 186.8 %all-gather.6.cloned.1.call-start = ((), (), s32[]{:S(2)}) async-start(), calls=%async_computation.5 | async-start | bytes 2359296 | tf_op jit(solution)/shard_map/all_gather | solution.py:121
  8.0 208.0 %all-gather.8.cloned.1.call-start = ((), (), s32[]{:S(2)}) async-start(), calls=%async_computation.6 | async-start | bytes 12582912 | tf_op jit(solution)/shard_map/all_gather | solution.py:125
  8.7 314.4 %all-gather.10.cloned.1.call-start = ((), (), s32[]{:S(2)}) async-start(), calls=%async_computation.7 | async-start | bytes 12582912 | tf_op jit(solution)/shard_map/all_gather | solution.py:137
  9.5 380.4 %reduce-scatter.10.cloned.1.call-start = ((), (), s32[]{:S(2)}) async-start(), calls=%async_computation.9 | async-start | bytes 786432 | tf_op jit(solution)/shard_map/reduce_scatter | solution.py:204
  9.5 339.4 %collective-permute-start = (bf16[4,1024,512]{2,1,0:T(8,128)(2,1)}, bf16[4,1024,512]{2,1,0:T(8,128)(2,1)}, u32[]{:S(2)}, u32[]{:S(2)}) collective-permute-start(bf16[4,1024,512]{2,1,0:T(8,128)(2,1)} %param.17), channel_id=1, source_target_pairs={{0,1},{1,0},{2,3},{3,2},{4,5},{5,4},{6,7},{7,6},{8,9},{9,8},{10,11... | collective-permute-start | bytes 12582920 | tf_op jit(solution)/shard_map/ppermute | solution.py:112
  197.4 0.7 copy-start.5
  200.2 122.9 %copy-start.8 = (f32[197,512]{1,0:T(8,128)S(1)}, f32[197,512]{1,0:T(8,128)}, u32[]{:S(2)}) copy-start(f32[197,512]{1,0:T(8,128)} %bitcast_convert_fusion) | copy-start | bytes 1210372
  323.1 6.4 copy-start.14
  340.8 7.4 copy-start.1
  340.8 8.1 copy-start.3
  340.9 8.1 copy-start.4
  348.9 9.7 %copy-start.12 = (bf16[1,197,512]{2,1,0:T(8,128)(2,1)S(1)}, bf16[1,197,512]{2,1,0:T(8,128)(2,1)}, u32[]{:S(2)}) copy-start(bf16[1,197,512]{2,1,0:T(8,128)(2,1)} %param.19) | copy-start | bytes 605188
  348.9 10.6 %copy-start.2 = (bf16[512,512]{1,0:T(8,128)(2,1)S(1)}, bf16[512,512]{1,0:T(8,128)(2,1)}, u32[]{:S(2)}) copy-start(bf16[512,512]{1,0:T(8,128)(2,1)} %all_gather.29) | copy-start | bytes 1572868
  348.9 11.6 %copy-start.6 = (bf16[8,64,197]{2,1,0:T(8,128)(2,1)S(1)}, bf16[8,64,197]{2,1,0:T(8,128)(2,1)}, u32[]{:S(2)}) copy-start(bf16[8,64,197]{2,1,0:T(8,128)(2,1)} %copy-done.5) | copy-start | bytes 605188
  365.9 43.6 %reduce-scatter.8.cloned.1.call-start = ((), (), s32[]{:S(2)}) async-start(), calls=%async_computation.8 | async-start | bytes 2359296 | tf_op jit(solution)/shard_map/reduce_scatter | solution.py:201
  366.0 2.6 copy-start.7
  371.1 140.5 %reduce-scatter.12.cloned.1.call-start = ((), (), s32[]{:S(2)}) async-start(), calls=%async_computation.10 | async-start | bytes 12582912 | tf_op jit(solution)/shard_map/reduce_scatter | solution.py:213
  379.3 1.0 copy-start.9
  379.3 234.5 %reduce-scatter.14.cloned.1.call-start = ((), (), s32[]{:S(2)}) async-start(), calls=%async_computation.11 | async-start | bytes 12582912 | tf_op jit(solution)/shard_map/reduce_scatter | solution.py:216
  388.2 225.6 %copy-start.18 = (u32[32]{0:T(128)S(1)}, u32[32]{0:T(128)}, u32[]{:S(2)}) copy-start(u32[32]{0:T(128)} %constant.120) | copy-start | bytes 388
  388.2 226.9 %copy-start.10 = (bf16[512,1536]{1,0:T(8,128)(2,1)S(1)}, bf16[512,1536]{1,0:T(8,128)(2,1)}, u32[]{:S(2)}) copy-start(bf16[512,1536]{1,0:T(8,128)(2,1)} %all-gather.6.cloned.1.call-done) | copy-start | bytes 4718596
  388.2 238.1 %reduce-scatter.16.cloned.1.call-start = ((), (), s32[]{:S(2)}) async-start(), calls=%async_computation.12 | async-start | bytes 196608
  389.8 426.6 %all-reduce.7.cloned.1.call-start = ((), (), s32[]{:S(2)}) async-start(), calls=%async_computation.13 | async-start | bytes 18874368 | tf_op jit(solution)/shard_map/psum | solution.py:226
Sparse Core Ops, SparseCore 0:
  9.6 46.8 all-gather.5
  58.1 157.8 all-gather.7
  217.6 105.4 all-gather.9
  366.0 14.5 reduce-scatter.9
  383.4 26.0 reduce-scatter.7
  412.3 99.2 reduce-scatter.11
  514.5 99.2 reduce-scatter.13
  616.0 10.2 reduce-scatter.15
  630.3 186.0 all-reduce.6
